TPU v7x, 32 devices: a whole 2x2x4 slice. The times are simulated.
32 devices in a mesh: prow: 8 (over y, x, core), pcol: 4 (over z).
Axes of the slice: x: 2, y: 2, z: 4, core: 2. Of those that a mesh axis runs over, the one named last changes fastest.
Arguments:
- inverse_trailing: bfloat16 [18432, 18432], P('prow', 'pcol'), may hold values from -6 to 6
- panel: bfloat16 [18432, 256], P('prow'), may hold values from -0.0625 to 0.0625
- supernode_inverse: float32 [256, 256], replicated, may hold values from -6 to 6
- block_live: int32 [72], replicated, may hold values from 0 to 1, as said below
Outputs:
- column_inverse: float32 [18432, 256], P('prow')
- diagonal_inverse: float32 [256, 256], replicated
Inputs may be any that keep to these rules, and one draw needn't show every extreme that they name: Each aligned group of 9 consecutive block rows (the rows of one index of prow) holds at least one block row with block_live 1.
All inputs are finite; a program needn't handle non-finite values.
Results may differ from a plain program's by a relative error of at most 0.0003.
Values may be sent and summed in bfloat16 or wider, within the bound.
No kernel may reach another device: no remote copies, remote signals or barrier semaphores. Data moves between devices by JAX's collectives and lax.ppermute only.
A program may use at most 128 MiB of HBM per device.

v0:
```python
import jax
import jax.numpy as jnp
from jax import lax
from jax.sharding import PartitionSpec as P


def from_root(block, axis, source):
    block = jnp.where(lax.axis_index(axis) == source, block, jnp.zeros_like(block))
    return lax.psum(block, axis)


def per_device(inverse_trailing, panel, supernode_inverse, block_live):
    rows_dev = panel.shape[0]
    width = panel.shape[1]
    col_count = inverse_trailing.shape[1]
    ratio = lax.axis_size("prow") // lax.axis_size("pcol")
    row_index = lax.axis_index("prow")
    col_index = lax.axis_index("pcol")
    live_all = jnp.repeat(block_live, width)
    col_live = lax.dynamic_slice_in_dim(live_all, col_index * col_count, col_count).astype(
        jnp.float32
    )
    row_live = lax.dynamic_slice_in_dim(live_all, row_index * rows_dev, rows_dev).astype(
        jnp.float32
    )
    partial_sum = jnp.zeros((rows_dev, width), jnp.float32)
    for half in range(ratio):
        received = from_root(panel, "prow", col_index * ratio + half)
        half_live = col_live[half * rows_dev : (half + 1) * rows_dev]
        masked_half = (received.astype(jnp.float32) * half_live[:, None]).astype(jnp.bfloat16)
        tile_cols = inverse_trailing[:, half * rows_dev : (half + 1) * rows_dev]
        partial_sum = partial_sum + jnp.dot(
            tile_cols, masked_half, preferred_element_type=jnp.float32
        )
    local_panel = panel.astype(jnp.float32) * row_live[:, None]
    contract_rows = (((0,), (0,)), ((), ()))
    total = lax.psum(partial_sum, "pcol")
    column_inverse = -total * row_live[:, None]
    term = lax.dot_general(
        local_panel, column_inverse, contract_rows, precision=lax.Precision.HIGHEST
    )
    diag_total = lax.psum(term, "prow")
    diagonal_inverse = supernode_inverse - diag_total
    return (column_inverse, diagonal_inverse)


def solution(mesh):
    in_specs = (P("prow", "pcol"), P("prow", None), P(), P())
    out_specs = (P("prow", None), P())
    return jax.shard_map(
        per_device, mesh=mesh, in_specs=in_specs, out_specs=out_specs, check_vma=False
    )
```

profile of v0, /device:TPU:0, one launch (start us, length us, event | category | flops | bytes accessed | tf_op | source)
XLA Modules:
  0.0 254.0 jit_solution(5009432006979550034)
XLA Ops:
  7.2 0.0 copy-start
  7.2 0.0 all-reduce.9.cloned.1.call-start
  7.2 2.8 %broadcast_select_fusion.1 = (bf16[2304,256]{1,0:T(8,128)(2,1)}, bf16[2304,256]{1,0:T(8,128)(2,1)}) fusion(bf16[2304,256]{1,0:T(8,128)(2,1)} %param.5, pred[]{:T(512)S(6)} %eq.6, pred[]{:T(512)S(6)} %eq.7), kind=kLoop, calls=%fused_computation.16 | loop fusion | flops 1179648 | bytes 3538946 | tf_op jit(solution)/shard_map/jit(_where)/select_n | solution.py:8
  10.1 0.0 all-reduce.9.cloned.1.call-update
  10.1 0.0 all-reduce.5.cloned.1.call-start
  10.2 0.0 copy-done
  10.2 0.1 broadcast_bitcast_fusion
  10.3 0.1 dynamic-slice_convert_fusion
  10.4 67.3 %all-reduce.9.cloned.1.call-done = (bf16[2304,256]{1,0:T(8,128)(2,1)}, bf16[2304,256]{1,0:T(8,128)(2,1)}) async-done(((bf16[2304,256]{1,0:T(8,128)(2,1)}, bf16[2304,256]{1,0:T(8,128)(2,1)}), (bf16[2304,256]{1,0:T(8,128)(2,1)}, bf16[2304,256]{1,0:T(8,128)(2,1)})) %all-reduce.9.cloned.1.call-update) | async-done | bytes 2359312 | tf_op jit(solution)/shard_map/psum | solution.py:9
  77.6 0.0 copy-start.3
  77.7 7.3 %fusion = f32[256,2304]{1,0:T(8,128)S(1)} fusion(bf16[2304,4608]{1,0:T(8,128)(2,1)} %param.4, bf16[2304,256]{1,0:T(8,128)(2,1)} %get-tuple-element.4, f32[2304]{0:T(1024)S(1)} %get-tuple-element.9), kind=kOutput, calls=%fused_computation | convolution fusion | flops 2719678464 | bytes 14164992 | tf_op jit(solution)/shard_map/dot_general | solution.py:32
  85.0 0.0 copy-done.3
  85.0 8.9 %fusion.7 = f32[2304,256]{0,1:T(8,128)} fusion(f32[256,2304]{1,0:T(8,128)S(1)} %fusion, bf16[2304,4608]{1,0:T(8,128)(2,1)} %param.4, bf16[2304,256]{1,0:T(8,128)(2,1)S(1)} %copy-done.3, f32[2304]{0:T(1024)S(1)} %get-tuple-element.8), kind=kOutput, calls=%fused_computation.5 | convolution fusion | flops 2720268288 | bytes 16524288 | tf_op jit(solution)/shard_map/dot_general | solution.py:32
  93.9 0.0 copy-start.1
  93.9 0.0 all-reduce.5.cloned.1.call-update
  93.9 0.0 all-reduce.7.cloned.1.call-start
  94.0 1.2 copy-done.1
  95.2 0.7 copy.6
  95.9 0.1 dynamic-slice_convert_fusion.1
  96.0 92.0 %all-reduce.5.cloned.1.call-done = f32[2304,256]{0,1:T(8,128)} async-done(((f32[2304,256]{0,1:T(8,128)}), f32[2304,256]{0,1:T(8,128)}) %all-reduce.5.cloned.1.call-update) | async-done | bytes 2359312 | tf_op jit(solution)/shard_map/psum | solution.py:37
  188.0 4.7 %fusion.10 = f32[256,256]{1,0:T(8,128)} fusion(bf16[2304,256]{0,1:T(8,128)(2,1)S(1)} %copy.6, f32[2304]{0:T(1024)S(1)} %dynamic-slice_convert_fusion.1, f32[2304,256]{0,1:T(8,128)} %all-reduce.5.cloned.1.call-done), kind=kOutput, calls=%fused_computation.6 | convolution fusion | flops 1814298624 | bytes 3810304 | tf_op jit(solution)/shard_map/dot_general | solution.py:39
  192.7 0.0 all-reduce.7.cloned.1.call-update
  192.7 1.8 negate_multiply_fusion
  194.6 0.0 copy-start.2
  194.6 2.0 copy.7
  196.5 49.3 %all-reduce.7.cloned.1.call-done = f32[256,256]{1,0:T(8,128)} async-done(((f32[256,256]{1,0:T(8,128)}), f32[256,256]{1,0:T(8,128)}) %all-reduce.7.cloned.1.call-update) | async-done | bytes 262160 | tf_op jit(solution)/shard_map/psum | solution.py:42
  245.8 0.0 copy-done.2
  245.8 1.7 sub.3
  (2 shorter events, 0.0 us)
Async XLA Ops:
  7.2 3.0 %copy-start = (s32[72]{0:T(128)S(1)}, s32[72]{0:T(128)}, u32[]{:S(2)}) copy-start(s32[72]{0:T(128)} %param.7) | copy-start | bytes 868
  7.2 70.5 %all-reduce.9.cloned.1.call-start = ((), (), s32[]{:S(2)}) async-start(), calls=%async_computation.2 | async-start | bytes 4718592 | tf_op jit(solution)/shard_map/psum | solution.py:9
  10.1 177.9 %all-reduce.5.cloned.1.call-start = ((), (), s32[]{:S(2)}) async-start(), calls=%async_computation | async-start | bytes 4718592 | tf_op jit(solution)/shard_map/psum | solution.py:37
  77.6 7.3 %copy-start.3 = (bf16[2304,256]{1,0:T(8,128)(2,1)S(1)}, bf16[2304,256]{1,0:T(8,128)(2,1)}, u32[]{:S(2)}) copy-start(bf16[2304,256]{1,0:T(8,128)(2,1)} %get-tuple-element.5) | copy-start | bytes 3538948
  93.9 1.3 copy-start.1
  93.9 151.9 %all-reduce.7.cloned.1.call-start = ((), (), s32[]{:S(2)}) async-start(), calls=%async_computation.1 | async-start | bytes 524288 | tf_op jit(solution)/shard_map/psum | solution.py:42
  194.6 51.2 %copy-start.2 = (f32[256,256]{1,0:T(8,128)S(1)}, f32[256,256]{1,0:T(8,128)}, u32[]{:S(2)}) copy-start(f32[256,256]{1,0:T(8,128)} %param.6) | copy-start | bytes 786436
Sparse Core Ops, SparseCore 0:
  11.9 65.7 all-reduce.8
  94.0 93.9 all-reduce.4
  192.9 52.9 all-reduce.6
where the time goes:
time: 254 us
  waiting for transfers between devices  209 us (82%)
  matrix products  20.9 us (8%)
  between operations  13.8 us (5%)
  other arithmetic  6.55 us (3%)
  local copies, waits for them, and re-layouts  4.01 us (2%)
    psum x1, waiting for transfers between devices, per_device(): total = lax.psum(partial_sum, 'pcol')  92 us
    psum x1, waiting for transfers between devices, from_root(): return lax.psum(block, axis)  67.3 us
    psum x1, waiting for transfers between devices, per_device(): diag_total = lax.psum(term, 'prow')  49.3 us
    dot_general x2, matrix products, per_device(): jnp.dot(tile_cols, masked_half, preferred_element_type=jnp.float32)  16.2 us
  transfers between devices with their start and end apart: 3, of which 3 were waited for; matrix products, arithmetic and copies ran while one was open for 2% of the time, Pallas kernels for 0%

commit v1 on v0

v1 whole, which is shorter than its diff:
```python
import functools

import jax
import jax.numpy as jnp
from jax import lax
from jax.experimental import pallas as pl
from jax.experimental.pallas import tpu as pltpu
from jax.sharding import PartitionSpec as P


AXES = ("prow", "pcol")
SMALLEST = 9
SCRATCH = 8 << 20
TAIL = 16
STEPS = 64.0
TOP = 32760.0
LN2 = 0.6931471805599453
F32 = jnp.float32
VMEM = pl.BlockSpec(memory_space=pltpu.VMEM)
SMEM = pl.BlockSpec(memory_space=pltpu.SMEM)
HBM = pl.BlockSpec(memory_space=pltpu.HBM)


def near(x):
    return pltpu.with_memory_space_constraint(x, pltpu.VMEM)


def kernel(body, outs, specs, out_specs, **options):
    params = pltpu.CompilerParams(vmem_limit_bytes=SCRATCH)
    return pl.pallas_call(
        body, out_shape=outs, in_specs=specs, out_specs=out_specs, compiler_params=params, **options
    )


def quantize(x):
    top = jnp.maximum(jnp.max(jnp.abs(x), axis=0, keepdims=True), 1e-30)
    step = jnp.ceil(jnp.log(top) * (STEPS / LN2))
    scale = jnp.exp(step * (-LN2 / STEPS)) * TOP
    return jnp.round(x * scale).astype(jnp.int32).astype(jnp.int16), step


def widen(q, step):
    return q.astype(jnp.int32).astype(F32) * (jnp.exp(step * (LN2 / STEPS)) * (1.0 / TOP))


def store_message(ref, blocks, size):
    steps = []
    for i, x in enumerate(blocks):
        q, step = quantize(x)
        ref[i * size : (i + 1) * size, :] = q
        steps.append(step)
    pad = jnp.zeros((TAIL - len(steps), ref.shape[1]), F32)
    tail = jnp.concatenate(steps + [pad], axis=0)
    ref[len(blocks) * size :, :] = tail.astype(jnp.int32).astype(jnp.int16)


def message_blocks(ref, size):
    count = (ref.shape[0] - TAIL) // size
    tail = ref[count * size :, :].astype(jnp.int32).astype(F32)
    return [widen(ref[i * size : (i + 1) * size, :], tail[i : i + 1, :]) for i in range(count)]


def is_middle(n_pcol):
    pcol = lax.axis_index("pcol")
    return jnp.logical_or(pcol == n_pcol // 2 - 1, pcol == n_pcol // 2)


def pack_kernel(live, panel, a, b, rows, cols, valid, *, n, per, ratio):
    size = panel.shape[0] // per
    split = a.shape[0] // size
    prow, pcol = lax.axis_index("prow"), lax.axis_index("pcol")
    core = prow % ratio
    a[...] = jnp.zeros_like(a)
    b[...] = jnp.zeros_like(b)
    for i in range(n):
        rows[i] = 0
        valid[i] = 0
        cols[i] = 0
        cols[n + i] = 0
    slot = 0
    for k in range(per):
        alive = live[prow * per + k] != 0

        @pl.when(alive)
        def _():
            rows[slot] = k
            valid[slot] = 1

        @pl.when(jnp.logical_and(alive, slot < split))
        def _():
            a[pl.ds(pl.multiple_of(slot * size, size), size), :] = panel[k * size : (k + 1) * size, :]

        @pl.when(jnp.logical_and(alive, slot >= split))
        def _():
            start = pl.multiple_of((slot - split) * size, size)
            b[pl.ds(start, size), :] = panel[k * size : (k + 1) * size, :]

        slot = slot + alive.astype(jnp.int32)
    for side in range(ratio):
        which = core if side == 0 else ratio - 1 - core
        slot = 0
        for k in range(per):
            alive = live[(pcol * ratio + which) * per + k] != 0

            @pl.when(alive)
            def _():
                cols[side * n + slot] = which * per + k

            slot = slot + alive.astype(jnp.int32)


def fetch_kernel(rows, cols, a, out, sem, *, first, size):
    for i in range(out.shape[0] // size):
        r = pl.multiple_of(rows[first + i] * size, size)

        def copy(j, _, i=i, r=r):
            c = pl.multiple_of(cols[j] * size, size)
            to = out.at[pl.ds(i * size, size), pl.ds(pl.multiple_of(j * size, size), size)]
            pltpu.make_async_copy(a.at[pl.ds(r, size), pl.ds(c, size)], to, sem).start()
            return 0

        lax.fori_loop(0, out.shape[1] // size, copy, 0, unroll=True)
    whole = a.at[pl.ds(0, out.shape[0]), pl.ds(0, out.shape[1])]
    pltpu.make_async_copy(whole, out, sem).wait()


def merge_kernel(a, xa, ya, da, b, xb, yb, db, full, *, ratio):
    root = lax.axis_index("prow") // ratio == lax.axis_index("pcol")
    top = a.shape[0]
    full[:top, :] = jnp.where(root, a[...], xa[...] + ya[...] + da[...])
    full[top:, :] = jnp.where(root, b[...], xb[...] + yb[...] + db[...])


def product_kernel(left, own, other, a, b, *refs, first, size):
    part, message, term = refs[-3:]
    n_rows = own.shape[0]
    acc = jnp.dot(left[:, :n_rows], own[...], preferred_element_type=F32)
    acc = acc + jnp.dot(left[:, n_rows:], other[...], preferred_element_type=F32)
    part[...] = acc
    count = left.shape[0] // size
    store_message(message, [acc[i * size : (i + 1) * size, :] for i in range(count)], size)
    contract = (((0,), (0,)), ((), ()))
    high = acc.astype(jnp.bfloat16)
    low = (acc - high.astype(F32)).astype(jnp.bfloat16)
    total = refs[0][...] if len(refs) == 4 else None
    split = a.shape[0] // size
    for i in range(count):
        at = first + i
        local = a[at * size : (at + 1) * size, :] if at < split else b[(at - split) * size : (at - split + 1) * size, :]
        for x in (high, low):
            piece = lax.dot_general(local, x[i * size : (i + 1) * size, :], contract, preferred_element_type=F32)
            total = piece if total is None else total + piece
    term[...] = total


def join_kernel(part, came, message, *, size):
    blocks = message_blocks(came, size)
    store_message(message, [part[i * size : (i + 1) * size, :] + x for i, x in enumerate(blocks)], size)


def meet_kernel(mine, came, message, *, size):
    pairs = zip(message_blocks(mine, size), message_blocks(came, size))
    store_message(message, [x + y for x, y in pairs], size)


def spread_kernel(rows, valid, live, total, came, *refs, first, size, per, n_pcol, fill):
    out, blocks, zeros, sem = refs[-4:]
    middle = is_middle(n_pcol)
    count = blocks.shape[0] // size
    prow = lax.axis_index("prow")

    def zero(k):
        return pltpu.make_async_copy(zeros, out.at[pl.ds(k * size, size), :], sem.at[count + k])

    def copy(i):
        start = pl.multiple_of(rows[first + i] * size, size)
        return pltpu.make_async_copy(blocks.at[pl.ds(i * size, size), :], out.at[pl.ds(start, size), :], sem.at[i])

    if fill:
        zeros[...] = jnp.zeros_like(zeros)
        for k in range(per):
            pl.when(live[prow * per + k] == 0)(lambda k=k: zero(k).start())
    picked = jnp.where(middle, total[...], came[...])
    tail = picked[count * size :, :].astype(jnp.int32).astype(F32)
    for i in range(count):
        blocks[i * size : (i + 1) * size, :] = -widen(picked[i * size : (i + 1) * size, :], tail[i : i + 1, :])
        pl.when(valid[first + i] != 0)(lambda i=i: copy(i).start())
    for i in range(count):
        pl.when(valid[first + i] != 0)(lambda i=i: copy(i).wait())
    if fill:
        for k in range(per):
            pl.when(live[prow * per + k] == 0)(lambda k=k: zero(k).wait())


def pick_kernel(total, came, out, *, n_pcol):
    out[...] = jnp.where(is_middle(n_pcol), total[...], came[...])


def add_kernel(x, y, out):
    out[...] = x[...] + y[...]


def halves_kernel(term, keep, give, *, ratio):
    core = lax.axis_index("prow") % ratio
    half = keep.shape[1]
    left, right = term[:, :half], term[:, half:]
    keep[...] = jnp.where(core == 0, left, right)
    give[...] = jnp.where(core == 0, right, left)


def root_kernel(a, b, out, *, ratio):
    root = lax.axis_index("prow") // ratio == lax.axis_index("pcol")
    top = a.shape[0]
    out[:top, :] = jnp.where(root, a[...], jnp.zeros_like(a))
    out[top:, :] = jnp.where(root, b[...], jnp.zeros_like(b))


def diagonal_kernel(base, mine, other, out, *, ratio):
    core = lax.axis_index("prow") % ratio
    half = out.shape[1] // ratio
    size = out.shape[0]
    left = jnp.where(core == 0, mine[...], other[...])
    right = jnp.where(core == 0, other[...], mine[...])
    for h, m in ((0, left), (1, right)):
        value = widen(m[:size, :], m[size : size + 1, :].astype(jnp.int32).astype(F32))
        out[:, h * half : (h + 1) * half] = base[:, h * half : (h + 1) * half] + value


def chunk_sizes(n):
    return {9: (2, 3, 2, 2), 8: (2, 2, 2, 2), 7: (2, 2, 2, 1), 6: (2, 2, 1, 1), 5: (2, 2, 1)}.get(n, (n,))


def packed_step(inverse_trailing, panel, supernode_inverse, block_live, *, n, n_prow, n_pcol):
    rows_dev, width = panel.shape
    per = block_live.shape[0] // n_prow
    size = rows_dev // per
    ratio = n_prow // n_pcol
    chips = n_prow // ratio

    def send(value, target):
        pairs = []
        for p in range(n_prow):
            for c in range(n_pcol):
                to = target(p, c)
                if to is not None:
                    pairs.append((p * n_pcol + c, to[0] * n_pcol + to[1]))
        return near(lax.ppermute(value, AXES, pairs))

    def place(p, c):
        return (p // ratio) ^ c

    inverse_trailing = pltpu.with_memory_space_constraint(inverse_trailing, pltpu.HBM)

    split = n - n // 2
    tables = [jax.ShapeDtypeStruct((k,), jnp.int32) for k in (n, 2 * n, n)]
    sides = [pltpu.VMEM((k * size, width), panel.dtype) for k in (split, n - split)]
    a, b, rows, cols, valid = kernel(
        functools.partial(pack_kernel, n=n, per=per, ratio=ratio),
        sides + tables, [SMEM, VMEM], [VMEM] * 2 + [SMEM] * 3,
    )(block_live, panel)

    def to_x(p, c):
        return (p ^ ratio, c)

    def to_y(p, c):
        return (p ^ (2 * ratio), c)

    def only(step, *places):
        return lambda p, c: step(p, c) if place(p, c) in places else None

    chunks = chunk_sizes(n)
    lefts = []
    first = 0
    for count in chunks:
        lefts.append(
            kernel(
                functools.partial(fetch_kernel, first=first, size=size),
                pltpu.VMEM((count * size, 2 * n * size), inverse_trailing.dtype), [SMEM, SMEM, HBM], VMEM,
                scratch_shapes=[pltpu.SemaphoreType.DMA],
            )(rows, cols, inverse_trailing)
        )
        first += count
    if chips == 4:
        xa = send(a, only(to_x, 0))
        yb = send(b, only(to_y, 0))
        xb = send(b, only(to_x, 0))
        ya = send(a, only(to_y, 0))
        da = send(xa, only(to_y, 1))
        db = send(yb, only(to_x, 2))
        own = kernel(
            functools.partial(merge_kernel, ratio=ratio),
            pltpu.VMEM((n * size, width), panel.dtype), [VMEM] * 8, VMEM,
        )(a, xa, ya, da, b, xb, yb, db)
    else:
        shape = pltpu.VMEM((n * size, width), panel.dtype)
        own = kernel(functools.partial(root_kernel, ratio=ratio), shape, [VMEM] * 2, VMEM)(a, b)
        bit = 1
        while bit < chips:
            def spread(p, c, bit=bit):
                return (p ^ (bit * ratio), c) if place(p, c) < bit else None

            own = kernel(add_kernel, shape, [VMEM] * 2, VMEM)(own, send(own, spread))
            bit *= 2
    swap = lambda p, c: (p ^ 1, c)
    other = send(own, swap)

    middle = n_pcol // 2

    def sum_over_line(part, message):
        out = pltpu.VMEM(message.shape, jnp.int16)
        for hop in range(middle - 1):
            def inwards(p, c, hop=hop):
                return {hop: (p, c + 1), n_pcol - 1 - hop: (p, c - 1)}.get(c)

            came = send(message, inwards)
            message = kernel(functools.partial(join_kernel, size=part_size), out, [VMEM] * 2, VMEM)(part, came)
        across = send(message, lambda p, c: (p, n_pcol - 1 - c) if c in (middle - 1, middle) else None)
        total = kernel(functools.partial(meet_kernel, size=part_size), out, [VMEM] * 2, VMEM)(message, across)
        came, value = None, total
        for hop in range(middle - 1):
            def outwards(p, c, hop=hop):
                return {middle - 1 - hop: (p, c - 1), middle + hop: (p, c + 1)}.get(c)

            value = send(value, outwards)
            came = value if came is None else kernel(add_kernel, out, [VMEM] * 2, VMEM)(came, value)
        return total, came

    part_size = size
    term, sums = None, []
    first = 0
    for k, count in enumerate(chunks):
        message_shape = (count * size + TAIL, width)
        part, message, term = kernel(
            functools.partial(product_kernel, first=first, size=size),
            [pltpu.VMEM((count * size, width), F32), pltpu.VMEM(message_shape, jnp.int16),
             pltpu.VMEM((width, width), F32)],
            [VMEM] * (5 if term is None else 6), [VMEM] * 3,
        )(lefts[k], own, other, a, b, *(() if term is None else (term,)))
        sums.append((first, count, *sum_over_line(part, message)))
        first += count

    half = width // ratio
    shape = pltpu.VMEM((width, half), F32)
    d, give = kernel(functools.partial(halves_kernel, ratio=ratio), [shape] * 2, [VMEM], [VMEM] * 2)(term)
    came = send(give, swap)
    step = ratio
    while True:
        d = kernel(add_kernel, shape, [VMEM] * 2, VMEM)(d, came)
        if step >= n_prow:
            break
        came = send(d, lambda p, c, step=step: (p ^ step, c))
        step *= 2
    part_size = width
    message = kernel(
        lambda x, o: store_message(o, [x[...]], width), pltpu.VMEM((width + TAIL, half), jnp.int16), [VMEM], VMEM
    )(d)
    total, came = sum_over_line(d, message)
    mine = kernel(
        functools.partial(pick_kernel, n_pcol=n_pcol), pltpu.VMEM(message.shape, jnp.int16), [VMEM] * 2, VMEM
    )(total, came)
    back = send(mine, swap)
    diagonal_inverse = kernel(
        functools.partial(diagonal_kernel, ratio=ratio), jax.ShapeDtypeStruct((width, width), F32), [VMEM] * 3, VMEM
    )(supernode_inverse, mine, back)

    result = None
    for first, count, total, came in sums:
        result = kernel(
            functools.partial(
                spread_kernel, first=first, size=size, per=per, n_pcol=n_pcol, fill=result is None
            ),
            jax.ShapeDtypeStruct((rows_dev, width), F32),
            [SMEM] * 3 + [VMEM] * 2 + ([] if result is None else [HBM]), HBM,
            scratch_shapes=[
                pltpu.VMEM((count * size, width), F32), pltpu.VMEM((size, width), F32),
                pltpu.SemaphoreType.DMA((count + per,)),
            ],
            input_output_aliases={} if result is None else {5: 0},
        )(rows, valid, block_live, total, came, *(() if result is None else (result,)))
    return result, diagonal_inverse


def solution(mesh):
    n_prow, n_pcol = mesh.shape["prow"], mesh.shape["pcol"]

    def per_device(inverse_trailing, panel, supernode_inverse, block_live):
        per = block_live.shape[0] // n_prow
        smallest = min(per, SMALLEST)

        def program(n):
            def run(*args):
                return packed_step(*args, n=n, n_prow=n_prow, n_pcol=n_pcol)

            return run

        programs = [program(n) for n in range(smallest, per + 1)]
        args = (inverse_trailing, panel, supernode_inverse, block_live)
        if len(programs) == 1:
            return programs[0](*args)
        counts = jnp.sum((block_live != 0).astype(jnp.int32).reshape(n_prow, per), axis=1)
        return lax.switch(jnp.max(counts) - smallest, programs, *args)

    in_specs = (P("prow", "pcol"), P("prow", None), P(), P())
    out_specs = (P("prow", None), P())
    return jax.shard_map(
        per_device, mesh=mesh, in_specs=in_specs, out_specs=out_specs, check_vma=False
    )
```

time: 254 us -> 131 us (0.52)
  waiting for transfers between devices: 209 us -> 50 us
  starting transfers between devices: 0.12 us -> 43.7 us
  Pallas kernels: 0 us -> 33.2 us
  matrix products: 20.9 us -> 0 us
  between operations: 13.8 us -> 1.14 us
  other arithmetic: 6.55 us -> 0 us
    psum x3 -> x0, waiting for transfers between devices: 209 us -> none  [the longest x1 92 us: per_device(): total = lax.psum(partial_sum, 'pcol')]
    ppermute x0 -> x26, waiting for transfers between devices: none -> 50 us  [send(): return near(lax.ppermute(value, AXES, pairs))]
    ppermute x0 -> x26, starting transfers between devices: none -> 43.7 us  [send(): return near(lax.ppermute(value, AXES, pairs))]
    pallas_call x0 -> x31, Pallas kernels: none -> 33.2 us  [the longest x4 15.1 us: packed_step(): kernel(functools.partial(fetch_kernel, first=first, size=size), pltpu.VME...]
    dot_general x3 -> x0, matrix products: 20.9 us -> none  [the longest x2 16.2 us: per_device(): jnp.dot(tile_cols, masked_half, preferred_element_type=jnp.float32)]
    select_n x1 -> x0, other arithmetic: 2.84 us -> none  [from_root(): jnp.where(lax.axis_index(axis) == source, block, jnp.zeros_like(block))]
  transfers between devices with their start and end apart: 3 -> 26, of which waited for: 3 -> 8; matrix products, arithmetic and copies ran while one was open for 2% -> 0% of each run, Pallas kernels for 0% -> 20%
where the time goes in v1:
time: 131 us; the launch traced here: 130 us
  waiting for transfers between devices  50 us (38%)
  starting transfers between devices  43.7 us (33%)
  Pallas kernels  33.2 us (25%)
  local copies, waits for them, and re-layouts  1.93 us (1%)
    ppermute x26, waiting for transfers between devices, send(): return near(lax.ppermute(value, AXES, pairs))  50 us
    ppermute x26, starting transfers between devices, send(): return near(lax.ppermute(value, AXES, pairs))  43.7 us
    pallas_call x4, Pallas kernels, packed_step(): kernel(functools.partial(fetch_kernel, first=first, size=size), pltpu.VME...  15.1 us
    pallas_call x4, Pallas kernels, packed_step(): kernel(functools.partial(product_kernel, first=first, size=size), [pltpu....  8.22 us
    pallas_call x4, Pallas kernels, packed_step(): kernel(functools.partial(spread_kernel, first=first, size=size, per=per,...  5.47 us
  transfers between devices with their start and end apart: 26, of which 8 were waited for; matrix products, arithmetic and copies ran while one was open for 0% of the time, Pallas kernels for 20%

profile of v1, /device:TPU:0, one launch (start us, length us, event | category | flops | bytes accessed | tf_op | source)
XLA Modules:
  0.0 130.0 jit_solution(13111327327312941270)
XLA Ops:
  0.6 1.3 copy-done
  1.9 0.7 copy-done.2
  2.6 1.4 %shard_map.59 = (bf16[1280,256]{1,0:T(8,128)(2,1)S(1)}, bf16[1024,256]{1,0:T(8,128)(2,1)S(1)}, s32[9]{0:T(128)S(1)}, s32[18]{0:T(128)S(1)}, s32[9]{0:T(128)S(1)}) custom-call(s32[72]{0:T(128)S(1)} %copy-done.2, bf16[2304,256]{1,0:T(8,128)(2,1)S(1)} %copy-done), custom_call_target="tpu_custom_call" | custom-call | tf_op jit(solution)/shard_map/pallas_call | solution.py:257
  4.0 4.9 %collective-permute-start = (bf16[1280,256]{1,0:T(8,128)(2,1)S(1)}, bf16[1280,256]{1,0:T(8,128)(2,1)S(1)}, u32[]{:S(2)}, u32[]{:S(2)}) collective-permute-start(bf16[1280,256]{1,0:T(8,128)(2,1)S(1)} %get-tuple-element.24.a), channel_id=1, source_target_pairs={{0,8},{4,12},{9,1},{13,5},{18,26},{22,30},{27,19},{31,23}} | collective-permute-start | bytes 1966088 | tf_op jit(solution)/shard_map/ppermute | solution.py:247
  8.9 1.3 %collective-permute-start.4 = (bf16[1024,256]{1,0:T(8,128)(2,1)S(1)}, bf16[1024,256]{1,0:T(8,128)(2,1)S(1)}, u32[]{:S(2)}, u32[]{:S(2)}) collective-permute-start(bf16[1024,256]{1,0:T(8,128)(2,1)S(1)} %get-tuple-element.25.b), channel_id=1, source_target_pairs={{0,16},{4,20},{9,25},{13,29},{18,2},{22,6},{27,11},{31,15}} | collective-permute-start | bytes 1572872 | tf_op jit(solution)/shard_map/ppermute | solution.py:247
  10.2 1.3 %collective-permute-start.1 = (bf16[1280,256]{1,0:T(8,128)(2,1)S(1)}, bf16[1280,256]{1,0:T(8,128)(2,1)S(1)}, u32[]{:S(2)}, u32[]{:S(2)}) collective-permute-start(bf16[1280,256]{1,0:T(8,128)(2,1)S(1)} %get-tuple-element.24.a), channel_id=1, source_target_pairs={{0,16},{4,20},{9,25},{13,29},{18,2},{22,6},{27,11},{31,15}} | collective-permute-start | bytes 1966088 | tf_op jit(solution)/shard_map/ppermute | solution.py:247
  11.5 11.3 %collective-permute-done.xa = bf16[1280,256]{1,0:T(8,128)(2,1)S(1)} collective-permute-done((bf16[1280,256]{1,0:T(8,128)(2,1)S(1)}, bf16[1280,256]{1,0:T(8,128)(2,1)S(1)}, u32[]{:S(2)}, u32[]{:S(2)}) %collective-permute-start) | collective-permute-done | bytes 655392 | tf_op jit(solution)/shard_map/ppermute | solution.py:247
  22.8 0.7 collective-permute-start.2
  23.5 5.0 %collective-permute-start.3 = (bf16[1024,256]{1,0:T(8,128)(2,1)S(1)}, bf16[1024,256]{1,0:T(8,128)(2,1)S(1)}, u32[]{:S(2)}, u32[]{:S(2)}) collective-permute-start(bf16[1024,256]{1,0:T(8,128)(2,1)S(1)} %get-tuple-element.25.b), channel_id=1, source_target_pairs={{0,8},{4,12},{9,1},{13,5},{18,26},{22,30},{27,19},{31,23}} | collective-permute-start | bytes 1572872 | tf_op jit(solution)/shard_map/ppermute | solution.py:247
  28.6 0.7 collective-permute-start.5
  29.3 9.6 %collective-permute-done.3.xb = bf16[1024,256]{1,0:T(8,128)(2,1)S(1)} collective-permute-done((bf16[1024,256]{1,0:T(8,128)(2,1)S(1)}, bf16[1024,256]{1,0:T(8,128)(2,1)S(1)}, u32[]{:S(2)}, u32[]{:S(2)}) %collective-permute-start.3) | collective-permute-done | bytes 524320 | tf_op jit(solution)/shard_map/ppermute | solution.py:247
  38.9 0.3 shard_map.61.own
  39.2 0.1 collective-permute-start.6
  39.2 3.3 %shard_map.64.left = bf16[512,4608]{1,0:T(8,128)(2,1)S(1)} custom-call(s32[9]{0:T(128)S(1)} %get-tuple-element.21.rows, s32[18]{0:T(128)S(1)} %get-tuple-element.23.cols, bf16[2304,4608]{1,0:T(8,128)(2,1)} %a.7), custom_call_target="tpu_custom_call" | custom-call | tf_op jit(solution)/shard_map/pallas_call | solution.py:276
  42.6 4.4 %shard_map.63.left = bf16[768,4608]{1,0:T(8,128)(2,1)S(1)} custom-call(s32[9]{0:T(128)S(1)} %get-tuple-element.21.rows, s32[18]{0:T(128)S(1)} %get-tuple-element.23.cols, bf16[2304,4608]{1,0:T(8,128)(2,1)} %a.7), custom_call_target="tpu_custom_call" | custom-call | tf_op jit(solution)/shard_map/pallas_call | solution.py:276
  47.0 1.9 %shard_map.65 = (f32[512,256]{1,0:T(8,128)S(1)}, s16[528,256]{1,0:T(8,128)(2,1)S(1)}, f32[256,256]{1,0:T(8,128)S(1)}) custom-call(bf16[512,4608]{1,0:T(8,128)(2,1)S(1)} %shard_map.64.left, bf16[2304,256]{1,0:T(8,128)(2,1)S(1)} %shard_map.61.own, bf16[2304,256]{1,0:T(8,128)(2,1)S(1)} %collective-permute-done.6.other, ...), custom_call_target="tpu_custom_call" | custom-call | tf_op jit(solution)/shard_map/pallas_call | solution.py:333
  48.9 2.6 %shard_map.66 = (f32[768,256]{1,0:T(8,128)S(1)}, s16[784,256]{1,0:T(8,128)(2,1)S(1)}, f32[256,256]{1,0:T(8,128)S(1)}) custom-call(bf16[768,4608]{1,0:T(8,128)(2,1)S(1)} %shard_map.63.left, bf16[2304,256]{1,0:T(8,128)(2,1)S(1)} %shard_map.61.own, bf16[2304,256]{1,0:T(8,128)(2,1)S(1)} %collective-permute-done.6.other, ...), custom_call_target="tpu_custom_call" | custom-call | tf_op jit(solution)/shard_map/pallas_call | solution.py:333
  51.5 5.0 %collective-permute-start.13 = (s16[784,256]{1,0:T(8,128)(2,1)S(1)}, s16[784,256]{1,0:T(8,128)(2,1)S(1)}, u32[]{:S(2)}, u32[]{:S(2)}) collective-permute-start(s16[784,256]{1,0:T(8,128)(2,1)S(1)} %get-tuple-element.34), channel_id=1, source_target_pairs={{0,1},{3,2},{4,5},{7,6},{8,9},{11,10},{12,13},{15,14},{16,17},{19,... | collective-permute-start | bytes 1204232 | tf_op jit(solution)/shard_map/ppermute | solution.py:247
  56.5 3.3 %shard_map.62.left = bf16[512,4608]{1,0:T(8,128)(2,1)S(1)} custom-call(s32[9]{0:T(128)S(1)} %get-tuple-element.21.rows, s32[18]{0:T(128)S(1)} %get-tuple-element.23.cols, bf16[2304,4608]{1,0:T(8,128)(2,1)} %a.7), custom_call_target="tpu_custom_call" | custom-call | tf_op jit(solution)/shard_map/pallas_call | solution.py:276
  59.9 4.1 %shard_map.60.left = bf16[512,4608]{1,0:T(8,128)(2,1)S(1)} custom-call(s32[9]{0:T(128)S(1)} %get-tuple-element.21.rows, s32[18]{0:T(128)S(1)} %get-tuple-element.23.cols, bf16[2304,4608]{1,0:T(8,128)(2,1)} %a.7), custom_call_target="tpu_custom_call" | custom-call | tf_op jit(solution)/shard_map/pallas_call | solution.py:276
  64.0 2.2 %collective-permute-start.16 = (s16[528,256]{1,0:T(8,128)(2,1)S(1)}, s16[528,256]{1,0:T(8,128)(2,1)S(1)}, u32[]{:S(2)}, u32[]{:S(2)}) collective-permute-start(s16[528,256]{1,0:T(8,128)(2,1)S(1)} %get-tuple-element.36), channel_id=1, source_target_pairs={{0,1},{3,2},{4,5},{7,6},{8,9},{11,10},{12,13},{15,14},{16,17},{19,... | collective-permute-start | bytes 811016 | tf_op jit(solution)/shard_map/ppermute | solution.py:247
  66.2 1.9 %shard_map.67 = (f32[512,256]{1,0:T(8,128)S(1)}, s16[528,256]{1,0:T(8,128)(2,1)S(1)}, f32[256,256]{1,0:T(8,128)S(1)}) custom-call(bf16[512,4608]{1,0:T(8,128)(2,1)S(1)} %shard_map.62.left, bf16[2304,256]{1,0:T(8,128)(2,1)S(1)} %shard_map.61.own, bf16[2304,256]{1,0:T(8,128)(2,1)S(1)} %collective-permute-done.6.other, ...), custom_call_target="tpu_custom_call" | custom-call | tf_op jit(solution)/shard_map/pallas_call | solution.py:333
  68.0 1.3 %collective-permute-start.10 = (s16[528,256]{1,0:T(8,128)(2,1)S(1)}, s16[528,256]{1,0:T(8,128)(2,1)S(1)}, u32[]{:S(2)}, u32[]{:S(2)}) collective-permute-start(s16[528,256]{1,0:T(8,128)(2,1)S(1)} %get-tuple-element.32), channel_id=1, source_target_pairs={{0,1},{3,2},{4,5},{7,6},{8,9},{11,10},{12,13},{15,14},{16,17},{19,... | collective-permute-start | bytes 811016 | tf_op jit(solution)/shard_map/ppermute | solution.py:247
  69.4 1.9 %shard_map.68 = (f32[512,256]{1,0:T(8,128)S(1)}, s16[528,256]{1,0:T(8,128)(2,1)S(1)}, f32[256,256]{1,0:T(8,128)S(1)}) custom-call(bf16[512,4608]{1,0:T(8,128)(2,1)S(1)} %shard_map.60.left, bf16[2304,256]{1,0:T(8,128)(2,1)S(1)} %shard_map.61.own, bf16[2304,256]{1,0:T(8,128)(2,1)S(1)} %collective-permute-done.6.other, ...), custom_call_target="tpu_custom_call" | custom-call | tf_op jit(solution)/shard_map/pallas_call | solution.py:333
  71.2 1.3 %collective-permute-start.7 = (s16[528,256]{1,0:T(8,128)(2,1)S(1)}, s16[528,256]{1,0:T(8,128)(2,1)S(1)}, u32[]{:S(2)}, u32[]{:S(2)}) collective-permute-start(s16[528,256]{1,0:T(8,128)(2,1)S(1)} %get-tuple-element.30), channel_id=1, source_target_pairs={{0,1},{3,2},{4,5},{7,6},{8,9},{11,10},{12,13},{15,14},{16,17},{19,... | collective-permute-start | bytes 811016 | tf_op jit(solution)/shard_map/ppermute | solution.py:247
  72.6 0.2 shard_map.73.mine
  72.8 0.7 collective-permute-start.14
  73.5 0.9 collective-permute-start.19
  74.4 1.0 collective-permute-done.19.y
  75.5 0.1 collective-permute-start.20
  75.5 0.2 shard_map.75.mine
  75.7 0.7 collective-permute-start.17
  76.4 2.2 %collective-permute-done.10.came = s16[528,256]{1,0:T(8,128)(2,1)S(1)} collective-permute-done((s16[528,256]{1,0:T(8,128)(2,1)S(1)}, s16[528,256]{1,0:T(8,128)(2,1)S(1)}, u32[]{:S(2)}, u32[]{:S(2)}) %collective-permute-start.10) | collective-permute-done | bytes 270368 | tf_op jit(solution)/shard_map/ppermute | solution.py:247
  78.6 0.2 shard_map.71.mine
  78.8 0.7 collective-permute-start.11
  79.5 4.9 %collective-permute-done.7.came = s16[528,256]{1,0:T(8,128)(2,1)S(1)} collective-permute-done((s16[528,256]{1,0:T(8,128)(2,1)S(1)}, s16[528,256]{1,0:T(8,128)(2,1)S(1)}, u32[]{:S(2)}, u32[]{:S(2)}) %collective-permute-start.7) | collective-permute-done | bytes 270368 | tf_op jit(solution)/shard_map/ppermute | solution.py:247
  84.4 0.2 shard_map.69.mine
  84.6 0.7 collective-permute-start.8
  85.3 0.0 copy-start.1
  85.3 1.9 %collective-permute-start.21 = (f32[256,128]{1,0:T(8,128)S(1)}, f32[256,128]{1,0:T(8,128)S(1)}, u32[]{:S(2)}, u32[]{:S(2)}) collective-permute-start(f32[256,128]{1,0:T(8,128)S(1)} %shard_map.83.x), channel_id=1, source_target_pairs={{0,16},{1,17},{2,18},{3,19},{4,20},{5,21},{6,22},{7,23},{8,24},{9,... | collective-permute-start | bytes 393224 | tf_op jit(solution)/shard_map/ppermute | solution.py:247
  87.3 0.3 shard_map.74.total
  87.6 0.0 copy-start.3
  87.6 1.3 collective-permute-start.15
  88.9 2.5 %collective-permute-done.21.y = f32[256,128]{1,0:T(8,128)S(1)} collective-permute-done((f32[256,128]{1,0:T(8,128)S(1)}, f32[256,128]{1,0:T(8,128)S(1)}, u32[]{:S(2)}, u32[]{:S(2)}) %collective-permute-start.21) | collective-permute-done | bytes 131104 | tf_op jit(solution)/shard_map/ppermute | solution.py:247
  91.4 0.1 shard_map.85
  91.4 6.9 %collective-permute-start.22 = (s16[272,128]{1,0:T(8,128)(2,1)S(1)}, s16[272,128]{1,0:T(8,128)(2,1)S(1)}, u32[]{:S(2)}, u32[]{:S(2)}) collective-permute-start(s16[272,128]{1,0:T(8,128)(2,1)S(1)} %shard_map.85), channel_id=1, source_target_pairs={{0,1},{3,2},{4,5},{7,6},{8,9},{11,10},{12,13},{15,14},{16,17},{19,... | collective-permute-start | bytes 208904 | tf_op jit(solution)/shard_map/ppermute | solution.py:247
  98.4 0.2 shard_map.76.total
  98.6 1.3 collective-permute-start.18
  99.9 0.2 shard_map.72.total
  100.1 1.3 collective-permute-start.12
  101.4 0.2 shard_map.70.total
  101.6 1.3 collective-permute-start.9
  103.0 0.1 shard_map.86.mine
  103.0 0.7 collective-permute-start.23
  103.7 0.1 shard_map.87.total
  103.8 1.3 collective-permute-start.24
  105.1 17.2 %collective-permute-done.24.came = s16[272,128]{1,0:T(8,128)(2,1)S(1)} collective-permute-done((s16[272,128]{1,0:T(8,128)(2,1)S(1)}, s16[272,128]{1,0:T(8,128)(2,1)S(1)}, u32[]{:S(2)}, u32[]{:S(2)}) %collective-permute-start.24) | collective-permute-done | bytes 69664 | tf_op jit(solution)/shard_map/ppermute | solution.py:247
  122.4 0.1 collective-permute-start.25
  122.5 1.2 collective-permute-done.25.other
  123.7 0.8 shard_map.89
  124.5 1.7 %shard_map.77.refs_0_ = f32[2304,256]{1,0:T(8,128)} custom-call(s32[9]{0:T(128)S(1)} %get-tuple-element.21.rows, s32[9]{0:T(128)S(1)} %get-tuple-element.22.valid, s32[72]{0:T(128)S(1)} %copy-done.3, s16[528,256]{1,0:T(8,128)(2,1)S(1)} %shard_map.76.total, s16[528,256]{1,0:T(8,128)(2,1)S(1)} %collective-permute-done.18.came), custom_call_target="tpu_custom_call" | custom-call | tf_op jit(solution)/shard_map/pallas_call | solution.py:368
  126.2 1.6 %shard_map.78.refs_0_ = f32[2304,256]{1,0:T(8,128)} custom-call(s32[9]{0:T(128)S(1)} %get-tuple-element.21.rows, s32[9]{0:T(128)S(1)} %get-tuple-element.22.valid, s32[72]{0:T(128)S(1)} %copy-done.3, s16[784,256]{1,0:T(8,128)(2,1)S(1)} %shard_map.74.total, s16[784,256]{1,0:T(8,128)(2,1)S(1)} %collective-permute-done.15.came, ...), custom_call_target="tpu_custom_call", output_to_operand_aliasing={{}: (5, {})} | custom-call | tf_op jit(solution)/shard_map/pallas_call | solution.py:368
  127.8 1.4 %shard_map.79.refs_0_ = f32[2304,256]{1,0:T(8,128)} custom-call(s32[9]{0:T(128)S(1)} %get-tuple-element.21.rows, s32[9]{0:T(128)S(1)} %get-tuple-element.22.valid, s32[72]{0:T(128)S(1)} %copy-done.3, s16[528,256]{1,0:T(8,128)(2,1)S(1)} %shard_map.72.total, s16[528,256]{1,0:T(8,128)(2,1)S(1)} %collective-permute-done.12.came, ...), custom_call_target="tpu_custom_call", output_to_operand_aliasing={{}: (5, {})} | custom-call | tf_op jit(solution)/shard_map/pallas_call | solution.py:368
  129.3 0.8 shard_map.80
  (27 shorter events, 0.2 us)
Async XLA Ops:
  0.6 1.3 copy-start
  1.9 0.7 copy-start.2
  4.0 18.8 %collective-permute-start = (bf16[1280,256]{1,0:T(8,128)(2,1)S(1)}, bf16[1280,256]{1,0:T(8,128)(2,1)S(1)}, u32[]{:S(2)}, u32[]{:S(2)}) collective-permute-start(bf16[1280,256]{1,0:T(8,128)(2,1)S(1)} %get-tuple-element.24.a), channel_id=1, source_target_pairs={{0,8},{4,12},{9,1},{13,5},{18,26},{22,30},{27,19},{31,23}} | collective-permute-start | bytes 1966088 | tf_op jit(solution)/shard_map/ppermute | solution.py:247
  8.9 19.7 %collective-permute-start.4 = (bf16[1024,256]{1,0:T(8,128)(2,1)S(1)}, bf16[1024,256]{1,0:T(8,128)(2,1)S(1)}, u32[]{:S(2)}, u32[]{:S(2)}) collective-permute-start(bf16[1024,256]{1,0:T(8,128)(2,1)S(1)} %get-tuple-element.25.b), channel_id=1, source_target_pairs={{0,16},{4,20},{9,25},{13,29},{18,2},{22,6},{27,11},{31,15}} | collective-permute-start | bytes 1572872 | tf_op jit(solution)/shard_map/ppermute | solution.py:247
  10.2 28.7 %collective-permute-start.1 = (bf16[1280,256]{1,0:T(8,128)(2,1)S(1)}, bf16[1280,256]{1,0:T(8,128)(2,1)S(1)}, u32[]{:S(2)}, u32[]{:S(2)}) collective-permute-start(bf16[1280,256]{1,0:T(8,128)(2,1)S(1)} %get-tuple-element.24.a), channel_id=1, source_target_pairs={{0,16},{4,20},{9,25},{13,29},{18,2},{22,6},{27,11},{31,15}} | collective-permute-start | bytes 1966088 | tf_op jit(solution)/shard_map/ppermute | solution.py:247
  22.8 16.1 %collective-permute-start.2 = (bf16[1280,256]{1,0:T(8,128)(2,1)S(1)}, bf16[1280,256]{1,0:T(8,128)(2,1)S(1)}, u32[]{:S(2)}, u32[]{:S(2)}) collective-permute-start(bf16[1280,256]{1,0:T(8,128)(2,1)S(1)} %collective-permute-done.xa), channel_id=1, source_target_pairs={{1,17},{5,21},{8,24},{12,28},{19,3},{23,7},{26,10},{30,14}} | collective-permute-start | bytes 1966088 | tf_op jit(solution)/shard_map/ppermute | solution.py:247
  23.5 15.3 %collective-permute-start.3 = (bf16[1024,256]{1,0:T(8,128)(2,1)S(1)}, bf16[1024,256]{1,0:T(8,128)(2,1)S(1)}, u32[]{:S(2)}, u32[]{:S(2)}) collective-permute-start(bf16[1024,256]{1,0:T(8,128)(2,1)S(1)} %get-tuple-element.25.b), channel_id=1, source_target_pairs={{0,8},{4,12},{9,1},{13,5},{18,26},{22,30},{27,19},{31,23}} | collective-permute-start | bytes 1572872 | tf_op jit(solution)/shard_map/ppermute | solution.py:247
  28.6 10.3 %collective-permute-start.5 = (bf16[1024,256]{1,0:T(8,128)(2,1)S(1)}, bf16[1024,256]{1,0:T(8,128)(2,1)S(1)}, u32[]{:S(2)}, u32[]{:S(2)}) collective-permute-start(bf16[1024,256]{1,0:T(8,128)(2,1)S(1)} %collective-permute-done.4.yb), channel_id=1, source_target_pairs={{2,10},{6,14},{11,3},{15,7},{16,24},{20,28},{25,17},{29,21}} | collective-permute-start | bytes 1572872 | tf_op jit(solution)/shard_map/ppermute | solution.py:247
  39.2 7.8 %collective-permute-start.6 = (bf16[2304,256]{1,0:T(8,128)(2,1)S(1)}, bf16[2304,256]{1,0:T(8,128)(2,1)S(1)}, u32[]{:S(2)}, u32[]{:S(2)}) collective-permute-start(bf16[2304,256]{1,0:T(8,128)(2,1)S(1)} %shard_map.61.own), channel_id=1, source_target_pairs={{0,4},{1,5},{2,6},{3,7},{4,0},{5,1},{6,2},{7,3},{8,12},{9,13},{10,... | collective-permute-start | bytes 3538952 | tf_op jit(solution)/shard_map/ppermute | solution.py:247
  51.5 21.0 %collective-permute-start.13 = (s16[784,256]{1,0:T(8,128)(2,1)S(1)}, s16[784,256]{1,0:T(8,128)(2,1)S(1)}, u32[]{:S(2)}, u32[]{:S(2)}) collective-permute-start(s16[784,256]{1,0:T(8,128)(2,1)S(1)} %get-tuple-element.34), channel_id=1, source_target_pairs={{0,1},{3,2},{4,5},{7,6},{8,9},{11,10},{12,13},{15,14},{16,17},{19,... | collective-permute-start | bytes 1204232 | tf_op jit(solution)/shard_map/ppermute | solution.py:247
  64.0 11.6 %collective-permute-start.16 = (s16[528,256]{1,0:T(8,128)(2,1)S(1)}, s16[528,256]{1,0:T(8,128)(2,1)S(1)}, u32[]{:S(2)}, u32[]{:S(2)}) collective-permute-start(s16[528,256]{1,0:T(8,128)(2,1)S(1)} %get-tuple-element.36), channel_id=1, source_target_pairs={{0,1},{3,2},{4,5},{7,6},{8,9},{11,10},{12,13},{15,14},{16,17},{19,... | collective-permute-start | bytes 811016 | tf_op jit(solution)/shard_map/ppermute | solution.py:247
  68.0 10.6 %collective-permute-start.10 = (s16[528,256]{1,0:T(8,128)(2,1)S(1)}, s16[528,256]{1,0:T(8,128)(2,1)S(1)}, u32[]{:S(2)}, u32[]{:S(2)}) collective-permute-start(s16[528,256]{1,0:T(8,128)(2,1)S(1)} %get-tuple-element.32), channel_id=1, source_target_pairs={{0,1},{3,2},{4,5},{7,6},{8,9},{11,10},{12,13},{15,14},{16,17},{19,... | collective-permute-start | bytes 811016 | tf_op jit(solution)/shard_map/ppermute | solution.py:247
  71.2 13.2 %collective-permute-start.7 = (s16[528,256]{1,0:T(8,128)(2,1)S(1)}, s16[528,256]{1,0:T(8,128)(2,1)S(1)}, u32[]{:S(2)}, u32[]{:S(2)}) collective-permute-start(s16[528,256]{1,0:T(8,128)(2,1)S(1)} %get-tuple-element.30), channel_id=1, source_target_pairs={{0,1},{3,2},{4,5},{7,6},{8,9},{11,10},{12,13},{15,14},{16,17},{19,... | collective-permute-start | bytes 811016 | tf_op jit(solution)/shard_map/ppermute | solution.py:247
  72.8 14.5 %collective-permute-start.14 = (s16[784,256]{1,0:T(8,128)(2,1)S(1)}, s16[784,256]{1,0:T(8,128)(2,1)S(1)}, u32[]{:S(2)}, u32[]{:S(2)}) collective-permute-start(s16[784,256]{1,0:T(8,128)(2,1)S(1)} %shard_map.73.mine), channel_id=1, source_target_pairs={{1,2},{2,1},{5,6},{6,5},{9,10},{10,9},{13,14},{14,13},{17,18},{18,... | collective-permute-start | bytes 1204232 | tf_op jit(solution)/shard_map/ppermute | solution.py:247
  73.5 1.9 %collective-permute-start.19 = (f32[256,128]{1,0:T(8,128)S(1)}, f32[256,128]{1,0:T(8,128)S(1)}, u32[]{:S(2)}, u32[]{:S(2)}) collective-permute-start(f32[256,128]{1,0:T(8,128)S(1)} %get-tuple-element.39), channel_id=1, source_target_pairs={{0,4},{1,5},{2,6},{3,7},{4,0},{5,1},{6,2},{7,3},{8,12},{9,13},{10,... | collective-permute-start | bytes 393224 | tf_op jit(solution)/shard_map/ppermute | solution.py:247
  75.5 9.8 %collective-permute-start.20 = (f32[256,128]{1,0:T(8,128)S(1)}, f32[256,128]{1,0:T(8,128)S(1)}, u32[]{:S(2)}, u32[]{:S(2)}) collective-permute-start(f32[256,128]{1,0:T(8,128)S(1)} %shard_map.82.x), channel_id=1, source_target_pairs={{0,8},{1,9},{2,10},{3,11},{4,12},{5,13},{6,14},{7,15},{8,0},{9,1},... | collective-permute-start | bytes 393224 | tf_op jit(solution)/shard_map/ppermute | solution.py:247
  75.7 22.7 %collective-permute-start.17 = (s16[528,256]{1,0:T(8,128)(2,1)S(1)}, s16[528,256]{1,0:T(8,128)(2,1)S(1)}, u32[]{:S(2)}, u32[]{:S(2)}) collective-permute-start(s16[528,256]{1,0:T(8,128)(2,1)S(1)} %shard_map.75.mine), channel_id=1, source_target_pairs={{1,2},{2,1},{5,6},{6,5},{9,10},{10,9},{13,14},{14,13},{17,18},{18,... | collective-permute-start | bytes 811016 | tf_op jit(solution)/shard_map/ppermute | solution.py:247
  78.8 21.1 %collective-permute-start.11 = (s16[528,256]{1,0:T(8,128)(2,1)S(1)}, s16[528,256]{1,0:T(8,128)(2,1)S(1)}, u32[]{:S(2)}, u32[]{:S(2)}) collective-permute-start(s16[528,256]{1,0:T(8,128)(2,1)S(1)} %shard_map.71.mine), channel_id=1, source_target_pairs={{1,2},{2,1},{5,6},{6,5},{9,10},{10,9},{13,14},{14,13},{17,18},{18,... | collective-permute-start | bytes 811016 | tf_op jit(solution)/shard_map/ppermute | solution.py:247
  84.6 16.8 %collective-permute-start.8 = (s16[528,256]{1,0:T(8,128)(2,1)S(1)}, s16[528,256]{1,0:T(8,128)(2,1)S(1)}, u32[]{:S(2)}, u32[]{:S(2)}) collective-permute-start(s16[528,256]{1,0:T(8,128)(2,1)S(1)} %shard_map.69.mine), channel_id=1, source_target_pairs={{1,2},{2,1},{5,6},{6,5},{9,10},{10,9},{13,14},{14,13},{17,18},{18,... | collective-permute-start | bytes 811016 | tf_op jit(solution)/shard_map/ppermute | solution.py:247
  85.3 38.4 %copy-start.1 = (f32[256,256]{1,0:T(8,128)S(1)}, f32[256,256]{1,0:T(8,128)}, u32[]{:S(2)}) copy-start(f32[256,256]{1,0:T(8,128)} %base.1) | copy-start | bytes 786436
  85.3 6.0 %collective-permute-start.21 = (f32[256,128]{1,0:T(8,128)S(1)}, f32[256,128]{1,0:T(8,128)S(1)}, u32[]{:S(2)}, u32[]{:S(2)}) collective-permute-start(f32[256,128]{1,0:T(8,128)S(1)} %shard_map.83.x), channel_id=1, source_target_pairs={{0,16},{1,17},{2,18},{3,19},{4,20},{5,21},{6,22},{7,23},{8,24},{9,... | collective-permute-start | bytes 393224 | tf_op jit(solution)/shard_map/ppermute | solution.py:247
  87.6 36.9 %copy-start.3 = (s32[72]{0:T(128)S(1)}, s32[72]{0:T(128)}, u32[]{:S(2)}) copy-start(s32[72]{0:T(128)} %live.9) | copy-start | bytes 868
  87.6 38.6 %collective-permute-start.15 = (s16[784,256]{1,0:T(8,128)(2,1)S(1)}, s16[784,256]{1,0:T(8,128)(2,1)S(1)}, u32[]{:S(2)}, u32[]{:S(2)}) collective-permute-start(s16[784,256]{1,0:T(8,128)(2,1)S(1)} %shard_map.74.total), channel_id=1, source_target_pairs={{1,0},{2,3},{5,4},{6,7},{9,8},{10,11},{13,12},{14,15},{17,16},{18,... | collective-permute-start | bytes 1204232 | tf_op jit(solution)/shard_map/ppermute | solution.py:247
  91.4 11.5 %collective-permute-start.22 = (s16[272,128]{1,0:T(8,128)(2,1)S(1)}, s16[272,128]{1,0:T(8,128)(2,1)S(1)}, u32[]{:S(2)}, u32[]{:S(2)}) collective-permute-start(s16[272,128]{1,0:T(8,128)(2,1)S(1)} %shard_map.85), channel_id=1, source_target_pairs={{0,1},{3,2},{4,5},{7,6},{8,9},{11,10},{12,13},{15,14},{16,17},{19,... | collective-permute-start | bytes 208904 | tf_op jit(solution)/shard_map/ppermute | solution.py:247
  98.6 25.9 %collective-permute-start.18 = (s16[528,256]{1,0:T(8,128)(2,1)S(1)}, s16[528,256]{1,0:T(8,128)(2,1)S(1)}, u32[]{:S(2)}, u32[]{:S(2)}) collective-permute-start(s16[528,256]{1,0:T(8,128)(2,1)S(1)} %shard_map.76.total), channel_id=1, source_target_pairs={{1,0},{2,3},{5,4},{6,7},{9,8},{10,11},{13,12},{14,15},{17,16},{18,... | collective-permute-start | bytes 811016 | tf_op jit(solution)/shard_map/ppermute | solution.py:247
  100.1 27.7 %collective-permute-start.12 = (s16[528,256]{1,0:T(8,128)(2,1)S(1)}, s16[528,256]{1,0:T(8,128)(2,1)S(1)}, u32[]{:S(2)}, u32[]{:S(2)}) collective-permute-start(s16[528,256]{1,0:T(8,128)(2,1)S(1)} %shard_map.72.total), channel_id=1, source_target_pairs={{1,0},{2,3},{5,4},{6,7},{9,8},{10,11},{13,12},{14,15},{17,16},{18,... | collective-permute-start | bytes 811016 | tf_op jit(solution)/shard_map/ppermute | solution.py:247
  101.6 27.6 %collective-permute-start.9 = (s16[528,256]{1,0:T(8,128)(2,1)S(1)}, s16[528,256]{1,0:T(8,128)(2,1)S(1)}, u32[]{:S(2)}, u32[]{:S(2)}) collective-permute-start(s16[528,256]{1,0:T(8,128)(2,1)S(1)} %shard_map.70.total), channel_id=1, source_target_pairs={{1,0},{2,3},{5,4},{6,7},{9,8},{10,11},{13,12},{14,15},{17,16},{18,... | collective-permute-start | bytes 811016 | tf_op jit(solution)/shard_map/ppermute | solution.py:247
  103.0 0.7 collective-permute-start.23
  103.8 18.5 %collective-permute-start.24 = (s16[272,128]{1,0:T(8,128)(2,1)S(1)}, s16[272,128]{1,0:T(8,128)(2,1)S(1)}, u32[]{:S(2)}, u32[]{:S(2)}) collective-permute-start(s16[272,128]{1,0:T(8,128)(2,1)S(1)} %shard_map.87.total), channel_id=1, source_target_pairs={{1,0},{2,3},{5,4},{6,7},{9,8},{10,11},{13,12},{14,15},{17,16},{18,... | collective-permute-start | bytes 208904 | tf_op jit(solution)/shard_map/ppermute | solution.py:247
  122.4 1.3 %collective-permute-start.25 = (s16[272,128]{1,0:T(8,128)(2,1)S(1)}, s16[272,128]{1,0:T(8,128)(2,1)S(1)}, u32[]{:S(2)}, u32[]{:S(2)}) collective-permute-start(s16[272,128]{1,0:T(8,128)(2,1)S(1)} %shard_map.88.mine), channel_id=1, source_target_pairs={{0,4},{1,5},{2,6},{3,7},{4,0},{5,1},{6,2},{7,3},{8,12},{9,13},{10,... | collective-permute-start | bytes 208904 | tf_op jit(solution)/shard_map/ppermute | solution.py:247
